TPU v7x, 32 devices: a whole 2x2x4 slice. The times are simulated.
32 devices in a mesh: sfc: 16 (over z, y, x), lev: 2 (over core).
Axes of the slice: x: 2, y: 2, z: 4, core: 2. Of those that a mesh axis runs over, the one named last changes fastest.
Arguments:
- air_state: float32 [24, 8, 32768], P(None, 'lev', 'sfc'), may hold values from -6 to 6
- metric: float32 [2, 2048], P(None, 'sfc'), may hold values from -5 to 5
- jacobian: float32 [2048], P('sfc'), may hold values from 0.25 to 4
- edge_nbr: int32 [4, 2048], P(None, 'sfc'), may hold values from 0 to 2047, as said below
- edge_side: int32 [4, 2048], P(None, 'sfc'), may hold values from 0 to 3
- coszen: float32 [32768], P('sfc'), may hold values from -1 to 1
- kappa_base: float32 [112], replicated, may hold values from 0.02 to 2
- band_kappa: float32 [112, 20], replicated, may hold values from 0.005 to 0.2
- solar_weight: float32 [112], replicated, may hold values from 0.5 to 2
- stretch_pos: int32 [32768], P('sfc'), may hold values from 0 to 32767, as said below
- stretch_src: int32 [32768], P('sfc'), may hold values from 0 to 32767, as said below
Outputs:
- new_state: float32 [24, 8, 32768], P(None, 'lev', 'sfc')
- surface_flux: float32 [32768], P(('sfc', 'lev'))
Inputs may be any that keep to these rules, and one draw needn't show every extreme that they name: edge_nbr[k, g] lies within 128 elements of g along the curve, cyclically over 2048 elements; that distance is reached. stretch_pos is a permutation of the columns and stretch_src its inverse; column c belongs to the stretch of device stretch_pos[c] // 2048; each device receives 2048 columns, at most 256 of them from one device, a bound reached in every draw; the columns that one device sends to one device take consecutive stretch positions. `stretch_src`: the inverse of stretch_pos.
All inputs are finite; a program needn't handle non-finite values.
Results may differ from a plain program's by a relative error of at most 0.0001.
Values sent between devices are 32-bit elements; how exact they have to be, the bound alone decides.
A program may use at most 64 MiB of HBM per device.

v0:
```python
import jax
import jax.numpy as jnp
import numpy as np
from jax import lax
from jax.sharding import PartitionSpec as P

NODES = 16
GBLOCK = 16
GLL_POINTS = np.array([-1.0, -1.0 / np.sqrt(5.0), 1.0 / np.sqrt(5.0), 1.0])
EDGE_NODES = np.array([[4, 8], [13, 14], [11, 7], [2, 1]], dtype=np.int32)
STEP_DYN = 0.2
DEPTH_UNIT = 0.05
HEAT_SCALE = 0.1
FLUX_SCALE = 0.02


def extended(cells, sides, width):
    for axis, dim in sides:
        count = lax.axis_size(axis)
        head = lax.slice_in_dim(cells, 0, width, axis=dim)
        tail = lax.slice_in_dim(cells, cells.shape[dim] - width, cells.shape[dim], axis=dim)
        cells = jnp.concatenate(
            [
                lax.ppermute(tail, axis, [(i, (i + 1) % count) for i in range(count)]),
                cells,
                lax.ppermute(head, axis, [((i + 1) % count, i) for i in range(count)]),
            ],
            axis=dim,
        )
    return cells


def derivative_numpy():
    spacing = GLL_POINTS[:, None] - GLL_POINTS[None, :]
    unit_diag = np.eye(4)
    safe_space = np.where(unit_diag > 0, 1.0, spacing)
    weights_row = np.prod(safe_space, axis=1)
    derivative = weights_row[:, None] / weights_row[None, :] / safe_space
    inverse_gap = np.where(unit_diag > 0, 0.0, 1.0 / safe_space)
    derivative = np.where(unit_diag > 0, inverse_gap.sum(axis=1)[:, None], derivative)
    return (np.kron(derivative, np.eye(4)), np.kron(np.eye(4), derivative))


def edge_tables():
    edge_flat = EDGE_NODES.reshape(-1)
    select_rows = np.zeros((8, 16))
    select_rows[np.arange(8), edge_flat] = 1.0
    keep_nodes = 1.0 - select_rows.sum(axis=0)
    return (select_rows, keep_nodes)


def advance(element_grid, metric, rows_i, rows_j, start):
    first_term = jnp.einsum("an,flne->flae", rows_i, element_grid, precision=lax.Precision.HIGHEST)
    second_term = jnp.einsum("an,flne->flae", rows_j, element_grid, precision=lax.Precision.HIGHEST)
    return start + STEP_DYN * (metric[0] * first_term + metric[1] * second_term)


def radiate(tracers, sun_angle, kappa_base, band_kappa, solar_weight):
    squares = tracers * tracers
    groups = kappa_base.shape[0] // GBLOCK
    level_count = tracers.shape[1]
    column_count = tracers.shape[2]

    def one_group(running, pieces):
        base_rate, rate_rows, bright = pieces
        absorb = (
            jnp.einsum("gt,tln->gln", rate_rows, squares, precision=lax.Precision.HIGHEST)
            + base_rate[:, None, None]
        )
        layer_depth = absorb * DEPTH_UNIT
        depth_above = jnp.cumsum(layer_depth, axis=1) - layer_depth
        heating = jnp.einsum(
            "g,gln->ln",
            bright,
            jnp.exp(-depth_above) * (1.0 - jnp.exp(-layer_depth)),
            precision=lax.Precision.HIGHEST,
        )
        ground = jnp.einsum(
            "g,gn->n",
            bright,
            jnp.exp(-(depth_above[:, -1] + layer_depth[:, -1])),
            precision=lax.Precision.HIGHEST,
        )
        return ((running[0] + heating, running[1] + ground), None)

    start_vals = (
        jnp.zeros((level_count, column_count), jnp.float32),
        jnp.zeros((column_count,), jnp.float32),
    )
    stacked = (
        kappa_base.reshape(groups, GBLOCK),
        band_kappa.reshape(groups, GBLOCK, -1),
        solar_weight.reshape(groups, GBLOCK),
    )
    (heating, ground), _ = lax.scan(one_group, start_vals, stacked)
    sun_height = jnp.maximum(sun_angle, 0.0)
    return (HEAT_SCALE * sun_height * heating, FLUX_SCALE * sun_height * ground)


def exchange_edges(edge_values, jacobian):
    elem_count = edge_values.shape[3]
    edge_rows = edge_values.reshape(-1, elem_count)
    edge_block = jnp.concatenate([edge_rows, jacobian[None, :]], axis=0)
    return extended(edge_block, (("sfc", 1),), elem_count)


def physics_levels(tracers, sun_angle, kappa_base, band_kappa, solar_weight):
    local_cols = tracers.shape[2]
    lev_devices = lax.axis_size("lev")
    part_cols = local_cols // lev_devices
    whole_column = lax.all_to_all(tracers, "lev", split_axis=2, concat_axis=1, tiled=True)
    sun_part = lax.dynamic_slice_in_dim(sun_angle, lax.axis_index("lev") * part_cols, part_cols)
    heating, ground = radiate(whole_column, sun_part, kappa_base, band_kappa, solar_weight)
    heat_back = lax.all_to_all(heating, "lev", split_axis=0, concat_axis=1, tiled=True)
    return (heat_back, ground)


def first_of_group(group_ids, values, group_count, sentinel):
    device_lane = jnp.arange(group_count, dtype=jnp.int32)
    member = group_ids[:, None] == device_lane[None, :]
    lowest = jnp.min(jnp.where(member, values[:, None], sentinel), axis=0)
    return values - jnp.sum(jnp.where(member, lowest[None, :], 0), axis=1)


def local(
    air_state,
    metric,
    jacobian,
    edge_nbr,
    edge_side,
    coszen,
    kappa_base,
    band_kappa,
    solar_weight,
    stretch_pos,
    stretch_src,
):
    field_count, level_count, local_cols = air_state.shape
    elem_count = local_cols // NODES
    table_i, table_j = derivative_numpy()
    select_np, keep_np = edge_tables()
    along_i = jnp.asarray(table_i, jnp.float32)
    along_j = jnp.asarray(table_j, jnp.float32)
    select_rows = jnp.asarray(select_np, jnp.float32)
    place_rows = jnp.asarray(select_np.T.copy(), jnp.float32)
    keep_nodes = jnp.asarray(keep_np, jnp.float32)
    element_grid = air_state.reshape(field_count, level_count, NODES, elem_count)
    advanced = advance(element_grid, metric, along_i, along_j, element_grid)
    edge_values = jnp.einsum(
        "an,flne->flae", select_rows, advanced, precision=lax.Precision.HIGHEST
    )
    padded = exchange_edges(edge_values, jacobian)
    sfc_devices = lax.axis_size("sfc")
    all_cols = local_cols * sfc_devices
    window_start = (lax.axis_index("sfc") - 1) * elem_count
    near_index = jnp.mod(edge_nbr - window_start, elem_count * sfc_devices)
    span_width = 3 * elem_count
    flip_pair = jnp.asarray(np.array([1, 0], dtype=np.int32))
    take_index = (2 * edge_side[:, None, :] + flip_pair[None, :, None]) * span_width + near_index[
        :, None, :
    ]
    far_rows = padded[:-1].reshape(field_count * level_count, 8 * span_width)
    far_values = jnp.take(far_rows, take_index.reshape(-1), axis=1).reshape(
        field_count, level_count, 8, elem_count
    )
    far_jac = jnp.take(padded[-1], near_index.reshape(-1)).reshape(4, 1, elem_count)
    far_jac = jnp.broadcast_to(far_jac, (4, 2, elem_count)).reshape(8, elem_count)
    summed = (jacobian * edge_values + far_jac * far_values) / (jacobian + far_jac)
    placed = jnp.einsum("ak,flke->flae", place_rows, summed, precision=lax.Precision.HIGHEST)
    dynamic = (advanced * keep_nodes[:, None] + placed).reshape(
        field_count, level_count, local_cols
    )
    capacity = 2 * local_cols // sfc_devices
    target_dev = stretch_pos // local_cols
    buffer_slot = first_of_group(target_dev, stretch_pos, sfc_devices, all_cols)
    flat_slot = target_dev * capacity + buffer_slot
    slot_column = (
        jnp.zeros((sfc_devices * capacity,), jnp.int32)
        .at[flat_slot]
        .set(jnp.arange(local_cols, dtype=jnp.int32))
    )
    source_dev = stretch_src // local_cols
    position_ids = jnp.arange(local_cols, dtype=jnp.int32)
    source_rank = first_of_group(source_dev, position_ids, sfc_devices, local_cols)
    recv_index = source_dev * capacity + source_rank
    tracer_count = field_count - 4
    tracer_rows = dynamic[4:].reshape(tracer_count * level_count, local_cols)
    sent_tracers = jnp.take(tracer_rows, slot_column, axis=1)
    sent_sun = jnp.take(coszen, slot_column)[None, :]
    got_tracers, got_sun = (
        lax.all_to_all(sent_tracers, "sfc", split_axis=1, concat_axis=1, tiled=True),
        lax.all_to_all(sent_sun, "sfc", split_axis=1, concat_axis=1, tiled=True),
    )
    stretch_tracers = jnp.take(got_tracers, recv_index, axis=1).reshape(
        tracer_count, level_count, local_cols
    )
    stretch_sun = jnp.take(got_sun[0], recv_index)
    heating, surface_flux = physics_levels(
        stretch_tracers, stretch_sun, kappa_base, band_kappa, solar_weight
    )
    position_of_slot = (
        jnp.zeros((sfc_devices * capacity,), jnp.int32).at[recv_index].set(position_ids)
    )
    returned = lax.all_to_all(
        jnp.take(heating, position_of_slot, axis=1), "sfc", split_axis=1, concat_axis=1, tiled=True
    )
    heat_cols = jnp.take(returned, flat_slot, axis=1)
    new_state = dynamic.at[2].add(heat_cols)
    return (new_state, surface_flux)


def solution(mesh):
    return jax.shard_map(
        local,
        mesh=mesh,
        in_specs=(
            P(None, "lev", "sfc"),
            P(None, "sfc"),
            P("sfc"),
            P(None, "sfc"),
            P(None, "sfc"),
            P("sfc"),
            P(),
            P(),
            P(),
            P("sfc"),
            P("sfc"),
        ),
        out_specs=(P(None, "lev", "sfc"), P(("sfc", "lev"))),
        check_vma=False,
    )
```

profile of v0, /device:TPU:0, one launch (start us, length us, event | category | flops | bytes accessed | tf_op | source)
XLA Modules:
  0.0 224.6 jit_solution(11954770912788300574)
XLA Ops:
  0.7 1.6 reshape.316
  2.3 0.8 convolution_multiply_fusion
  3.1 0.9 fusion.25
  4.6 3.0 %collective-permute-start = (f32[769,128]{1,0:T(8,128)S(1)}, f32[769,128]{1,0:T(8,128)S(1)}, u32[]{:S(2)}, u32[]{:S(2)}) collective-permute-start(f32[769,128]{1,0:T(8,128)S(1)} %pad_maximum_fusion.3), channel_id=1, source_target_pairs={{0,2},{2,4},{4,6},{6,8},{8,10},{10,12},{12,14},{14,16},{16,18},{18... | collective-permute-start | bytes 1181192 | tf_op jit(solution)/shard_map/ppermute | solution.py:24
  7.6 4.1 %collective-permute-start.1 = (f32[769,128]{1,0:T(8,128)S(1)}, f32[769,128]{1,0:T(8,128)S(1)}, u32[]{:S(2)}, u32[]{:S(2)}) collective-permute-start(f32[769,128]{1,0:T(8,128)S(1)} %pad_maximum_fusion.3), channel_id=1, source_target_pairs={{2,0},{4,2},{6,4},{8,6},{10,8},{12,10},{14,12},{16,14},{18,16},{20... | collective-permute-start | bytes 1181192 | tf_op jit(solution)/shard_map/ppermute | solution.py:26
  12.5 8.1 %scatter_custom_fusion.1 = s32[4096]{0:T(1024)S(1)} fusion(s32[2048]{0:T(1024)S(1)} %get-tuple-element.93, s32[2048]{0:T(1024)S(1)} %iota.18, s32[]{:T(128)} %constant.211.clone.1), kind=kCustom, calls=%fused_computation.97 | custom fusion | bytes 16388 | tf_op jit(solution)/shard_map/scatter | solution.py:180
  20.6 23.0 %gather_fusion.2 = f32[4096]{0:T(1024)S(1)} fusion(f32[2048]{0:T(1024)S(1)} %copy-done, s32[4096]{0:T(1024)S(1)} %fusion.40), kind=kCustom, calls=%fused_computation.2 | custom fusion | bytes 49152 | tf_op jit(solution)/shard_map/jit(_take)/gather | solution.py:189
  44.3 3.4 %all-to-all-start = ((f32[1,16,256]{2,0,1:T(1,128)}), f32[1,16,256]{2,0,1:T(1,128)S(1)}, u32[]{:S(2)}, u32[]{:S(2)}) async-start(f32[1,16,256]{2,0,1:T(1,128)} %bitcast.24), calls=%async_computation | async-start | bytes 32768 | tf_op jit(solution)/shard_map/all_to_all | solution.py:192
  48.1 3.5 %gather_fusion = f32[512]{0:T(512)S(1)} fusion(f32[384]{0:T(512)S(1)} %maximum_reduce_fusion, s32[1024]{0:T(1024)S(1)} %pad_clamp_fusion), kind=kCustom, calls=%fused_computation | custom fusion | bytes 6144 | tf_op jit(solution)/shard_map/jit(_take)/gather | solution.py:166
  51.7 1.1 pad_maximum_fusion
  52.8 1.2 reshape.319
  54.0 1.7 copy.77
  55.8 2.8 %gather_fusion.1 = f32[1024,96]{1,0:T(8,128)S(1)} fusion(f32[96,3072]{0,1:T(8,128)S(1)} %copy.77, s32[1024]{0:T(1024)S(1)} %broadcast_clamp_fusion.2), kind=kCustom, calls=%fused_computation.1 | custom fusion | bytes 790528 | tf_op jit(solution)/shard_map/jit(_take)/gather | solution.py:163
  59.3 0.8 fusion.26
  61.3 10.8 %gather_fusion.4 = f32[4096,80]{1,0:T(8,128)S(1)} fusion(f32[80,2048]{0,1:T(8,128)S(1)} %copy.80, s32[4096]{0:T(1024)S(1)} %fusion.40), kind=kCustom, calls=%fused_computation.4 | custom fusion | bytes 2637824 | tf_op jit(solution)/shard_map/jit(_take)/gather | solution.py:188
  72.1 1.7 copy.81
  73.8 2.5 %broadcast_select_fusion = f32[80,16,256]{2,0,1:T(8,128)} fusion(f32[80,16,256]{2,0,1:T(8,128)} %copy.81, pred[16,256]{1,0:T(8,128)(4,1)S(1)} %broadcast_in_dim.170), kind=kLoop, calls=%fused_computation.50 | loop fusion | flops 327680 | bytes 2625536 | tf_op jit(solution)/shard_map/jit(_take)/select_n | solution.py:188
  76.4 7.0 %all-to-all-start.1 = ((f32[80,16,256]{2,0,1:T(8,128)}), f32[80,16,256]{2,0,1:T(8,128)S(1)}, u32[]{:S(2)}, u32[]{:S(2)}) async-start(f32[80,16,256]{2,0,1:T(8,128)} %broadcast_select_fusion), calls=%async_computation.1 | async-start | bytes 2621440 | tf_op jit(solution)/shard_map/all_to_all | solution.py:191
  85.1 8.2 %scatter_custom_fusion = s32[4096]{0:T(1024)S(1)} fusion(s32[2048]{0:T(1024)S(1)} %get-tuple-element.97, s32[2048]{0:T(1024)S(1)} %iota.17, s32[]{:T(128)} %constant.211.clone.1), kind=kCustom, calls=%fused_computation.99 | custom fusion | bytes 16388 | tf_op jit(solution)/shard_map/scatter | solution.py:202
  94.0 11.8 %gather_fusion.3 = f32[2048]{0:T(1024)S(1)} fusion(f32[4096]{0:T(1024)S(1)} %bitcast.132, s32[2048]{0:T(1024)S(1)} %broadcast_clamp_fusion.1), kind=kCustom, calls=%fused_computation.3 | custom fusion | bytes 24576 | tf_op jit(solution)/shard_map/jit(_take)/gather | solution.py:197
  105.8 6.5 %all-to-all-done.1 = f32[80,16,256]{2,0,1:T(8,128)S(1)} async-done(((f32[80,16,256]{2,0,1:T(8,128)}), f32[80,16,256]{2,0,1:T(8,128)S(1)}, u32[]{:S(2)}, u32[]{:S(2)}) %all-to-all-start.1) | async-done | bytes 1310752 | tf_op jit(solution)/shard_map/all_to_all | solution.py:191
  112.3 0.8 copy.82
  113.1 5.5 %gather_fusion.5 = f32[2048,80]{1,0:T(8,128)S(1)} fusion(f32[80,4096]{0,1:T(8,128)S(1)} %bitcast.134, s32[2048]{0:T(1024)S(1)} %broadcast_clamp_fusion.1), kind=kCustom, calls=%fused_computation.5 | custom fusion | bytes 1318912 | tf_op jit(solution)/shard_map/jit(_take)/gather | solution.py:194
  119.5 3.2 %copy.84 = f32[20,4,2048]{0,1,2:T(4,128)} copy(f32[20,4,2048]{2,1,0:T(4,128)S(1)} %broadcast_select_fusion.1) | data formatting | bytes 1310720 | tf_op jit(solution)/shard_map/jit(_take)/select_n | solution.py:194
  122.6 7.2 %reshape.428 = f32[2,1,81920]{2,1,0:T(1,128)S(1)} reshape(f32[2048,4,20]{2,1,0:T(4,128)} %bitcast.135) | data formatting | bytes 1310720
  129.9 4.3 %all_to_all.52 = f32[2,1,81920]{2,1,0:T(1,128)S(1)} all-to-all(f32[2,1,81920]{2,1,0:T(1,128)S(1)} %reshape.428), channel_id=1, replica_groups=mesh['sfc'=16,'lev'=2] {'lev'}, dimensions={0} | all-to-all | bytes 1310720 | tf_op jit(solution)/shard_map/all_to_all | solution.py:111
  134.7 2.6 %reduce.4 = f32[2,81920]{1,0:T(2,128)S(1)} reduce(f32[2,1,81920]{2,1,0:T(1,128)S(1)} %all_to_all.52, f32[]{:T(128)} %broadcast.316), dimensions={1}, to_apply=%all_to_all.40.reduce_sub_computation | reduce | bytes 1310724 | tf_op jit(solution)/shard_map/all_to_all | solution.py:111
  137.3 8.0 %reshape.429 = f32[2048,4,20]{2,1,0:T(4,128)} reshape(f32[2,81920]{1,0:T(2,128)S(1)} %reduce.4) | data formatting | bytes 1310720
  145.3 3.9 %bitcast_multiply_fusion.1 = f32[20,4,2048]{0,1,2:T(4,128)} fusion(f32[2048,4,20]{2,1,0:T(4,128)} %reshape.429), kind=kLoop, calls=%fused_computation.129 | loop fusion | flops 163840 | bytes 1310720 | tf_op jit(solution)/shard_map/mul | solution.py:59
  149.2 3.5 %copy.85 = f32[20,2,4,1024]{3,0,2,1:T(8,128)S(1)} copy(f32[20,2,4,1024]{0,2,3,1:T(4,128)} %bitcast.136) | data formatting | bytes 1310720 | tf_op jit(solution)/shard_map/mul | solution.py:59
  152.7 29.1 %while.14 = (s32[]{:T(128)}, f32[8,1024]{1,0:T(8,128)S(1)}, f32[1024]{0:T(1024)S(1)}, f32[7,16]{1,0:T(8,128)S(1)}, f32[7,16,20]{2,1,0:T(8,128)S(1)}, /*index=5*/...) while((s32[]{:T(128)}, f32[8,1024]{1,0:T(8,128)S(1)}, f32[1024]{0:T(1024)S(1)}, ...), condition=%wide.region_8.9_spmd.clone, body=%wide.region_6.8_spmd.clone.sunk | while | flops 35112960 | bytes 3696376 | solution.py:95
  154.0 2.1 reduce-window_subtract_fusion.2
  156.9 0.7 fusion.82
  158.2 2.1 reduce-window_subtract_fusion.2
  162.3 2.1 reduce-window_subtract_fusion.2
  165.2 0.7 fusion.82
  166.5 2.1 reduce-window_subtract_fusion.2
  170.6 2.1 reduce-window_subtract_fusion.2
  173.5 0.7 fusion.82
  174.8 2.1 reduce-window_subtract_fusion.2
  178.9 2.1 reduce-window_subtract_fusion.2
  182.4 3.7 %all_to_all.53 = f32[2,4,1024]{2,1,0:T(4,128)S(1)} all-to-all(f32[2,4,1024]{2,1,0:T(4,128)S(1)} %all_to_all.41), channel_id=1, replica_groups=mesh['sfc'=16,'lev'=2] {'lev'}, dimensions={0} | all-to-all | bytes 65536 | tf_op jit(solution)/shard_map/all_to_all | solution.py:114
  186.6 14.1 %gather_fusion.6 = f32[4096,4]{1,0:T(8,128)} fusion(f32[4,2048]{0,1:T(8,128)S(1)} %bitcast.145, s32[4096]{0:T(1024)S(1)} %fusion.39), kind=kCustom, calls=%fused_computation.6 | custom fusion | bytes 147456 | tf_op jit(solution)/shard_map/jit(_take)/gather | solution.py:205
  200.7 2.2 copy.87
  203.6 6.4 %all-to-all-start.4 = ((f32[4,16,256]{2,0,1:T(4,128)}), f32[4,16,256]{2,0,1:T(4,128)S(1)}, u32[]{:S(2)}, u32[]{:S(2)}) async-start(f32[4,16,256]{2,0,1:T(4,128)} %broadcast_select_fusion.2), calls=%async_computation.4 | async-start | bytes 131072 | tf_op jit(solution)/shard_map/all_to_all | solution.py:204
  210.0 1.1 reshape.320
  211.1 6.3 %all-to-all-done.4 = f32[4,16,256]{2,0,1:T(4,128)S(1)} async-done(((f32[4,16,256]{2,0,1:T(4,128)}), f32[4,16,256]{2,0,1:T(4,128)S(1)}, u32[]{:S(2)}, u32[]{:S(2)}) %all-to-all-start.4) | async-done | bytes 65568 | tf_op jit(solution)/shard_map/all_to_all | solution.py:204
  218.1 5.5 %gather_fusion.7 = f32[2048,4]{1,0:T(8,128)S(1)} fusion(f32[4,4096]{0,1:T(8,128)S(1)} %bitcast.142, s32[2048]{0:T(1024)S(1)} %broadcast_clamp_fusion), kind=kCustom, calls=%fused_computation.7 | custom fusion | bytes 73728 | tf_op jit(solution)/shard_map/jit(_take)/gather | solution.py:207
  (148 shorter events, 22.8 us)
Async XLA Ops:
  0.6 19.9 %copy-start = (f32[2048]{0:T(1024)S(1)}, f32[2048]{0:T(1024)}, u32[]{:S(2)}) copy-start(f32[2048]{0:T(1024)} %param.26) | copy-start | bytes 24580
  0.6 1.6 copy-start.10
  0.7 2.4 %copy-start.13 = (f32[16,16,1,1]{1,0,3,2:T(8,128)S(1)}, f32[16,16,1,1]{1,0,3,2:T(8,128)}, u32[]{:S(2)}) copy-start(f32[16,16,1,1]{1,0,3,2:T(8,128)} %constant.237) | copy-start | bytes 3076
  0.7 1.6 copy-start.18
  3.1 0.9 copy-start.15
  3.1 1.4 copy-start.8
  4.0 7.7 %copy-start.4 = (s32[2048]{0:T(1024)S(1)}, s32[2048]{0:T(1024)}, u32[]{:S(2)}) copy-start(s32[2048]{0:T(1024)} %param.30) | copy-start | bytes 24580
  4.6 43.5 %collective-permute-start = (f32[769,128]{1,0:T(8,128)S(1)}, f32[769,128]{1,0:T(8,128)S(1)}, u32[]{:S(2)}, u32[]{:S(2)}) collective-permute-start(f32[769,128]{1,0:T(8,128)S(1)} %pad_maximum_fusion.3), channel_id=1, source_target_pairs={{0,2},{2,4},{4,6},{6,8},{8,10},{10,12},{12,14},{14,16},{16,18},{18... | collective-permute-start | bytes 1181192 | tf_op jit(solution)/shard_map/ppermute | solution.py:24
  7.6 40.5 %collective-permute-start.1 = (f32[769,128]{1,0:T(8,128)S(1)}, f32[769,128]{1,0:T(8,128)S(1)}, u32[]{:S(2)}, u32[]{:S(2)}) collective-permute-start(f32[769,128]{1,0:T(8,128)S(1)} %pad_maximum_fusion.3), channel_id=1, source_target_pairs={{2,0},{4,2},{6,4},{8,6},{10,8},{12,10},{14,12},{16,14},{18,16},{20... | collective-permute-start | bytes 1181192 | tf_op jit(solution)/shard_map/ppermute | solution.py:26
  20.6 27.1 %copy-start.11 = (s32[4,128]{1,0:T(4,128)S(1)}, s32[4,128]{1,0:T(4,128)}, u32[]{:S(2)}) copy-start(s32[4,128]{1,0:T(4,128)} %param.24) | copy-start | bytes 6148
  20.6 27.2 %copy-start.17 = (s32[4,128]{1,0:T(4,128)S(1)}, s32[4,128]{1,0:T(4,128)}, u32[]{:S(2)}) copy-start(s32[4,128]{1,0:T(4,128)} %param.25) | copy-start | bytes 6148
  20.6 27.2 %copy-start.16 = (s32[2]{0:T(128)S(1)}, s32[2]{0:T(128)}, u32[]{:S(2)}) copy-start(s32[2]{0:T(128)} %constant.236.clone) | copy-start | bytes 28
  44.3 32.1 %all-to-all-start = ((f32[1,16,256]{2,0,1:T(1,128)}), f32[1,16,256]{2,0,1:T(1,128)S(1)}, u32[]{:S(2)}, u32[]{:S(2)}) async-start(f32[1,16,256]{2,0,1:T(1,128)} %bitcast.24), calls=%async_computation | async-start | bytes 32768 | tf_op jit(solution)/shard_map/all_to_all | solution.py:192
  48.1 3.5 %copy-start.3 = (f32[769,128]{1,0:T(8,128)}, f32[769,128]{1,0:T(8,128)S(1)}, u32[]{:S(2)}) copy-start(f32[769,128]{1,0:T(8,128)S(1)} %collective-permute-done.1) | copy-start | bytes 1181188
  58.6 0.7 copy-start.14
  58.6 0.7 copy-start.21
  60.1 0.9 copy-start.1
  76.3 7.1 %copy-start.9 = (f32[112,20]{0,1:T(8,128)S(1)}, f32[112,20]{0,1:T(8,128)}, u32[]{:S(2)}) copy-start(f32[112,20]{0,1:T(8,128)} %param.28) | copy-start | bytes 26884
  76.3 7.2 %copy-start.19 = (f32[112]{0:T(128)S(1)}, f32[112]{0:T(128)}, u32[]{:S(2)}) copy-start(f32[112]{0:T(128)} %param.29) | copy-start | bytes 1348
  76.3 7.3 %copy-start.20 = (f32[112]{0:T(128)S(1)}, f32[112]{0:T(128)}, u32[]{:S(2)}) copy-start(f32[112]{0:T(128)} %param.27) | copy-start | bytes 1348
  76.3 7.9 %copy-start.5 = (s32[2048]{0:T(1024)S(1)}, s32[2048]{0:T(1024)}, u32[]{:S(2)}) copy-start(s32[2048]{0:T(1024)} %param.31) | copy-start | bytes 24580
  76.4 36.0 %all-to-all-start.1 = ((f32[80,16,256]{2,0,1:T(8,128)}), f32[80,16,256]{2,0,1:T(8,128)S(1)}, u32[]{:S(2)}, u32[]{:S(2)}) async-start(f32[80,16,256]{2,0,1:T(8,128)} %broadcast_select_fusion), calls=%async_computation.1 | async-start | bytes 2621440 | tf_op jit(solution)/shard_map/all_to_all | solution.py:191
  118.6 0.7 copy-start.7
  186.5 16.3 %copy-start.6 = (pred[16,256]{1,0:T(8,128)(4,1)S(1)}, pred[16,256]{1,0:T(8,128)(4,1)}, u32[]{:S(2)}) copy-start(pred[16,256]{1,0:T(8,128)(4,1)} %broadcast_in_dim.162) | copy-start | bytes 12292
  186.6 23.4 %copy-start.2 = (f32[24,4,16,128]{3,2,1,0:T(8,128)S(1)}, f32[24,4,16,128]{3,2,1,0:T(8,128)}, u32[]{:S(2)}) copy-start(f32[24,4,16,128]{3,2,1,0:T(8,128)} %copy-done.1) | copy-start | bytes 2359300
  200.7 10.4 %slice-start = ((f32[24,4,16,128]{3,2,1,0:T(8,128)}), f32[1,4,16,128]{3,2,1,0:T(8,128)S(1)}, s32[]{:S(2)}) async-start(f32[24,4,16,128]{3,2,1,0:T(8,128)} %copy-done.1), calls=%async_computation.5 | async-start | bytes 65536 | tf_op jit(solution)/shard_map/slice.28
  203.6 13.9 %all-to-all-start.4 = ((f32[4,16,256]{2,0,1:T(4,128)}), f32[4,16,256]{2,0,1:T(4,128)S(1)}, u32[]{:S(2)}, u32[]{:S(2)}) async-start(f32[4,16,256]{2,0,1:T(4,128)} %broadcast_select_fusion.2), calls=%async_computation.4 | async-start | bytes 131072 | tf_op jit(solution)/shard_map/all_to_all | solution.py:204
  211.1 12.8 %copy-start.12 = (pred[2048]{0:T(1024)(128)(4,1)S(1)}, pred[2048]{0:T(1024)(128)(4,1)}, u32[]{:S(2)}) copy-start(pred[2048]{0:T(1024)(128)(4,1)} %get-tuple-element.92) | copy-start | bytes 6148
where the time goes:
time: 226 us; the launch traced here: 225 us
  local copies, waits for them, and re-layouts  136 us (60%)
  other arithmetic  30 us (13%)
  starting transfers between devices  23.9 us (11%)
  waiting for transfers between devices  12.9 us (6%)
  matrix products  11.6 us (5%)
  blocking collectives  8.01 us (4%)
    gather x1, local copies, waits for them, and re-layouts, local(): sent_sun = jnp.take(coszen, slot_column)[None, :]  23 us
    unnamed x49, local copies, waits for them, and re-layouts  16.8 us
    gather x2, local copies, waits for them, and re-layouts, local(): jnp.take(heating, position_of_slot, axis=1)  16.3 us
    another operation x7, other arithmetic, one_group(): depth_above = jnp.cumsum(layer_depth, axis=1) - layer_depth  15 us
    gather x2, local copies, waits for them, and re-layouts, local(): sent_tracers = jnp.take(tracer_rows, slot_column, axis=1)  12.5 us
    gather x1, local copies, waits for them, and re-layouts, local(): stretch_sun = jnp.take(got_sun[0], recv_index)  11.8 us
    scatter x1, local copies, waits for them, and re-layouts, local(): jnp.zeros((sfc_devices * capacity,), jnp.int32).at[recv_index]  8.24 us
    scatter x1, local copies, waits for them, and re-layouts, local(): slot_column = jnp.zeros((sfc_devices * capacity,), jnp.int32).at[flat_slo...  8.06 us
  transfers between devices with their start and end apart: 5, of which 2 were waited for; matrix products, arithmetic and copies ran while one was open for 37% of the time, Pallas kernels for 0%

commit v1 on v0

--- a/solution.py
+++ b/solution.py
@@ -201,8 +201,16 @@
     position_of_slot = (
         jnp.zeros((sfc_devices * capacity,), jnp.int32).at[recv_index].set(position_ids)
     )
-    returned = lax.all_to_all(
-        jnp.take(heating, position_of_slot, axis=1), "sfc", split_axis=1, concat_axis=1, tiled=True
+    returned = jnp.concatenate(
+        lax.all_to_all(
+            jnp.stack(
+                jnp.split(jnp.take(heating, position_of_slot, axis=1), lax.axis_size("sfc"), axis=1)
+            ),
+            "sfc",
+            0,
+            0,
+        ),
+        axis=1,
     )
     heat_cols = jnp.take(returned, flat_slot, axis=1)
     new_state = dynamic.at[2].add(heat_cols)

time: 226 us -> 233 us (1.031)
  waiting for transfers between devices: 12.9 us -> 22 us
  local copies, waits for them, and re-layouts: 136 us -> 132 us
    all_to_all x1, waiting for transfers between devices: 6.53 us -> 15.6 us  [local(): lax.all_to_all(sent_tracers, 'sfc', split_axis=1, concat_axis=1, tiled=True)]
    gather x2 -> x1, local copies, waits for them, and re-layouts: 16.3 us -> 10.8 us  [local(): jnp.take(heating, position_of_slot, axis=1)]
    unnamed x49 -> x68, local copies, waits for them, and re-layouts: 16.8 us -> 16.7 us
  transfers between devices with their start and end apart: 5 -> 5, of which waited for: 2 -> 2; matrix products, arithmetic and copies ran while one was open for 37% -> 36% of each run, Pallas kernels for 0% -> 0%
where the time goes in v1:
time: 233 us; the launch traced here: 232 us
  local copies, waits for them, and re-layouts  132 us (57%)
  other arithmetic  32.2 us (14%)
  starting transfers between devices  23.8 us (10%)
  waiting for transfers between devices  22 us (9%)
  matrix products  12.3 us (5%)
  blocking collectives  8.01 us (3%)
    gather x1, local copies, waits for them, and re-layouts, local(): sent_sun = jnp.take(coszen, slot_column)[None, :]  23 us
    unnamed x68, local copies, waits for them, and re-layouts  16.7 us
    all_to_all x1, waiting for transfers between devices, local(): lax.all_to_all(sent_tracers, 'sfc', split_axis=1, concat_axis=1, tiled=True)  15.6 us
    another operation x7, other arithmetic, one_group(): depth_above = jnp.cumsum(layer_depth, axis=1) - layer_depth  15 us
    gather x2, local copies, waits for them, and re-layouts, local(): sent_tracers = jnp.take(tracer_rows, slot_column, axis=1)  12.5 us
    gather x1, local copies, waits for them, and re-layouts, local(): stretch_sun = jnp.take(got_sun[0], recv_index)  11.8 us
    gather x1, local copies, waits for them, and re-layouts, local(): jnp.take(heating, position_of_slot, axis=1)  10.8 us
    scatter x1, local copies, waits for them, and re-layouts, local(): slot_column = jnp.zeros((sfc_devices * capacity,), jnp.int32).at[flat_slo...  8.06 us
  transfers between devices with their start and end apart: 5, of which 2 were waited for; matrix products, arithmetic and copies ran while one was open for 36% of the time, Pallas kernels for 0%

profile of v1, /device:TPU:0, one launch (start us, length us, event | category | flops | bytes accessed | tf_op | source)
XLA Modules:
  0.0 232.2 jit_solution(16023395014770243272)
XLA Ops:
  0.7 1.5 reshape.314
  2.2 0.8 slice_bitcast_fusion.17
  3.0 1.5 convolution_multiply_fusion
  4.5 0.9 fusion.25
  6.0 3.0 %collective-permute-start = (f32[769,128]{1,0:T(8,128)S(1)}, f32[769,128]{1,0:T(8,128)S(1)}, u32[]{:S(2)}, u32[]{:S(2)}) collective-permute-start(f32[769,128]{1,0:T(8,128)S(1)} %pad_maximum_fusion.3), channel_id=1, source_target_pairs={{0,2},{2,4},{4,6},{6,8},{8,10},{10,12},{12,14},{14,16},{16,18},{18... | collective-permute-start | bytes 1181192 | tf_op jit(solution)/shard_map/ppermute | solution.py:24
  9.0 4.1 %collective-permute-start.1 = (f32[769,128]{1,0:T(8,128)S(1)}, f32[769,128]{1,0:T(8,128)S(1)}, u32[]{:S(2)}, u32[]{:S(2)}) collective-permute-start(f32[769,128]{1,0:T(8,128)S(1)} %pad_maximum_fusion.3), channel_id=1, source_target_pairs={{2,0},{4,2},{6,4},{8,6},{10,8},{12,10},{14,12},{16,14},{18,16},{20... | collective-permute-start | bytes 1181192 | tf_op jit(solution)/shard_map/ppermute | solution.py:26
  14.8 8.1 %scatter_custom_fusion = s32[4096]{0:T(1024)S(1)} fusion(s32[2048]{0:T(1024)S(1)} %get-tuple-element.97, s32[2048]{0:T(1024)S(1)} %iota.17, s32[]{:T(128)} %constant.211.clone.1), kind=kCustom, calls=%fused_computation.131 | custom fusion | bytes 16388 | tf_op jit(solution)/shard_map/scatter | solution.py:202
  22.9 8.1 %scatter_custom_fusion.1 = s32[4096]{0:T(1024)S(1)} fusion(s32[2048]{0:T(1024)S(1)} %get-tuple-element.93, s32[2048]{0:T(1024)S(1)} %iota.18, s32[]{:T(128)} %constant.211.clone.1), kind=kCustom, calls=%fused_computation.129 | custom fusion | bytes 16388 | tf_op jit(solution)/shard_map/scatter | solution.py:180
  31.0 23.0 %gather_fusion.2 = f32[4096]{0:T(1024)S(1)} fusion(f32[2048]{0:T(1024)S(1)} %copy-done, s32[4096]{0:T(1024)S(1)} %get-tuple-element.103), kind=kCustom, calls=%fused_computation.2 | custom fusion | bytes 49152 | tf_op jit(solution)/shard_map/jit(_take)/gather | solution.py:189
  54.6 3.5 %all-to-all-start = ((f32[1,16,256]{2,0,1:T(1,128)}), f32[1,16,256]{2,0,1:T(1,128)S(1)}, u32[]{:S(2)}, u32[]{:S(2)}) async-start(f32[1,16,256]{2,0,1:T(1,128)} %bitcast.24), calls=%async_computation | async-start | bytes 32768 | tf_op jit(solution)/shard_map/all_to_all | solution.py:192
  58.6 3.5 %gather_fusion = f32[512]{0:T(512)S(1)} fusion(f32[384]{0:T(512)S(1)} %maximum_reduce_fusion, s32[1024]{0:T(1024)S(1)} %pad_clamp_fusion), kind=kCustom, calls=%fused_computation | custom fusion | bytes 6144 | tf_op jit(solution)/shard_map/jit(_take)/gather | solution.py:166
  62.1 1.1 pad_maximum_fusion
  63.2 1.2 reshape.317
  64.5 1.7 copy.109
  66.2 2.8 %gather_fusion.1 = f32[1024,96]{1,0:T(8,128)S(1)} fusion(f32[96,3072]{0,1:T(8,128)S(1)} %copy.109, s32[1024]{0:T(1024)S(1)} %broadcast_clamp_fusion.2), kind=kCustom, calls=%fused_computation.1 | custom fusion | bytes 790528 | tf_op jit(solution)/shard_map/jit(_take)/gather | solution.py:163
  69.3 0.8 fusion.26
  71.4 10.8 %gather_fusion.4 = f32[4096,80]{1,0:T(8,128)S(1)} fusion(f32[80,2048]{0,1:T(8,128)S(1)} %copy.112, s32[4096]{0:T(1024)S(1)} %get-tuple-element.103), kind=kCustom, calls=%fused_computation.4 | custom fusion | bytes 2637824 | tf_op jit(solution)/shard_map/jit(_take)/gather | solution.py:188
  82.2 1.7 copy.113
  83.9 2.6 %broadcast_select_fusion = f32[80,16,256]{2,0,1:T(8,128)} fusion(f32[80,16,256]{2,0,1:T(8,128)} %copy.113, pred[16,256]{1,0:T(8,128)(4,1)S(1)} %broadcast_in_dim.167), kind=kLoop, calls=%fused_computation.51 | loop fusion | flops 327680 | bytes 2625536 | tf_op jit(solution)/shard_map/jit(_take)/select_n | solution.py:188
  86.5 6.9 %all-to-all-start.1 = ((f32[80,16,256]{2,0,1:T(8,128)}), f32[80,16,256]{2,0,1:T(8,128)S(1)}, u32[]{:S(2)}, u32[]{:S(2)}) async-start(f32[80,16,256]{2,0,1:T(8,128)} %broadcast_select_fusion), calls=%async_computation.1 | async-start | bytes 2621440 | tf_op jit(solution)/shard_map/all_to_all | solution.py:191
  94.9 11.8 %gather_fusion.3 = f32[2048]{0:T(1024)S(1)} fusion(f32[4096]{0:T(1024)S(1)} %bitcast.196, s32[2048]{0:T(1024)S(1)} %broadcast_clamp_fusion.1), kind=kCustom, calls=%fused_computation.3 | custom fusion | bytes 24576 | tf_op jit(solution)/shard_map/jit(_take)/gather | solution.py:197
  106.6 15.6 %all-to-all-done.1 = f32[80,16,256]{2,0,1:T(8,128)S(1)} async-done(((f32[80,16,256]{2,0,1:T(8,128)}), f32[80,16,256]{2,0,1:T(8,128)S(1)}, u32[]{:S(2)}, u32[]{:S(2)}) %all-to-all-start.1) | async-done | bytes 1310752 | tf_op jit(solution)/shard_map/all_to_all | solution.py:191
  122.3 0.8 copy.114
  123.1 5.5 %gather_fusion.5 = f32[2048,80]{1,0:T(8,128)S(1)} fusion(f32[80,4096]{0,1:T(8,128)S(1)} %bitcast.198, s32[2048]{0:T(1024)S(1)} %broadcast_clamp_fusion.1), kind=kCustom, calls=%fused_computation.5 | custom fusion | bytes 1318912 | tf_op jit(solution)/shard_map/jit(_take)/gather | solution.py:194
  129.5 3.2 %copy.116 = f32[20,4,2048]{0,1,2:T(4,128)} copy(f32[20,4,2048]{2,1,0:T(4,128)S(1)} %broadcast_select_fusion.1) | data formatting | bytes 1310720 | tf_op jit(solution)/shard_map/jit(_take)/select_n | solution.py:194
  132.6 7.2 %reshape.428 = f32[2,1,81920]{2,1,0:T(1,128)S(1)} reshape(f32[2048,4,20]{2,1,0:T(4,128)} %bitcast.199) | data formatting | bytes 1310720
  139.9 4.3 %all_to_all.48 = f32[2,1,81920]{2,1,0:T(1,128)S(1)} all-to-all(f32[2,1,81920]{2,1,0:T(1,128)S(1)} %reshape.428), channel_id=1, replica_groups=mesh['sfc'=16,'lev'=2] {'lev'}, dimensions={0} | all-to-all | bytes 1310720 | tf_op jit(solution)/shard_map/all_to_all | solution.py:111
  144.7 2.7 %reduce.4 = f32[2,81920]{1,0:T(2,128)S(1)} reduce(f32[2,1,81920]{2,1,0:T(1,128)S(1)} %all_to_all.48, f32[]{:T(128)} %broadcast.319), dimensions={1}, to_apply=%all_to_all.37.reduce_sub_computation | reduce | bytes 1310724 | tf_op jit(solution)/shard_map/all_to_all | solution.py:111
  147.4 8.0 %reshape.429 = f32[2048,4,20]{2,1,0:T(4,128)} reshape(f32[2,81920]{1,0:T(2,128)S(1)} %reduce.4) | data formatting | bytes 1310720
  155.4 3.9 %bitcast_multiply_fusion.1 = f32[20,4,2048]{0,1,2:T(4,128)} fusion(f32[2048,4,20]{2,1,0:T(4,128)} %reshape.429), kind=kLoop, calls=%fused_computation.161 | loop fusion | flops 163840 | bytes 1310720 | tf_op jit(solution)/shard_map/mul | solution.py:59
  159.3 3.5 %copy.117 = f32[20,2,4,1024]{3,0,2,1:T(8,128)S(1)} copy(f32[20,2,4,1024]{0,2,3,1:T(4,128)} %bitcast.200) | data formatting | bytes 1310720 | tf_op jit(solution)/shard_map/mul | solution.py:59
  162.8 29.1 %while.14 = (s32[]{:T(128)}, f32[8,1024]{1,0:T(8,128)S(1)}, f32[1024]{0:T(1024)S(1)}, f32[7,16]{1,0:T(8,128)S(1)}, f32[7,16,20]{2,1,0:T(8,128)S(1)}, /*index=5*/...) while((s32[]{:T(128)}, f32[8,1024]{1,0:T(8,128)S(1)}, f32[1024]{0:T(1024)S(1)}, ...), condition=%wide.region_8.9_spmd.clone, body=%wide.region_6.8_spmd.clone.sunk | while | flops 35112960 | bytes 3696376 | solution.py:95
  164.1 2.1 reduce-window_subtract_fusion.2
  167.0 0.7 fusion.98
  168.3 2.1 reduce-window_subtract_fusion.2
  172.4 2.1 reduce-window_subtract_fusion.2
  176.6 2.1 reduce-window_subtract_fusion.2
  180.7 2.1 reduce-window_subtract_fusion.2
  184.9 2.1 reduce-window_subtract_fusion.2
  189.1 2.1 reduce-window_subtract_fusion.2
  192.6 3.7 %all_to_all.49 = f32[2,4,1024]{2,1,0:T(4,128)S(1)} all-to-all(f32[2,4,1024]{2,1,0:T(4,128)S(1)} %all_to_all.38), channel_id=1, replica_groups=mesh['sfc'=16,'lev'=2] {'lev'}, dimensions={0} | all-to-all | bytes 65536 | tf_op jit(solution)/shard_map/all_to_all | solution.py:114
  196.7 10.8 %gather_fusion.6 = f32[4096,4]{1,0:T(8,128)S(1)} fusion(f32[4,2048]{0,1:T(8,128)S(1)} %bitcast.209, s32[4096]{0:T(1024)S(1)} %get-tuple-element.102), kind=kCustom, calls=%fused_computation.6 | custom fusion | bytes 147456 | tf_op jit(solution)/shard_map/jit(_take)/gather | solution.py:207
  207.5 2.1 select_bitcast_fusion
  210.0 1.2 copy.119
  211.2 6.4 %all-to-all-start.4 = ((f32[16,4,256]{2,1,0:T(4,128)}), f32[16,4,256]{2,1,0:T(4,128)S(1)}, u32[]{:S(2)}, u32[]{:S(2)}) async-start(f32[16,4,256]{2,1,0:T(4,128)} %copy.119), calls=%async_computation.4 | async-start | bytes 131072 | tf_op jit(solution)/shard_map/all_to_all | solution.py:205
  217.6 1.1 reshape.318
  218.8 6.3 %all-to-all-done.4 = f32[16,4,256]{2,1,0:T(4,128)S(1)} async-done(((f32[16,4,256]{2,1,0:T(4,128)}), f32[16,4,256]{2,1,0:T(4,128)S(1)}, u32[]{:S(2)}, u32[]{:S(2)}) %all-to-all-start.4) | async-done | bytes 65568 | tf_op jit(solution)/shard_map/all_to_all | solution.py:205
  225.8 5.5 %gather_fusion.7 = f32[2048,4]{1,0:T(8,128)S(1)} fusion(f32[4,4096]{0,1:T(8,128)S(1)} %bitcast.206, s32[2048]{0:T(1024)S(1)} %broadcast_clamp_fusion), kind=kCustom, calls=%fused_computation.7 | custom fusion | bytes 73728 | tf_op jit(solution)/shard_map/jit(_take)/gather | solution.py:215
  (166 shorter events, 23.4 us)
Async XLA Ops:
  0.6 30.3 %copy-start = (f32[2048]{0:T(1024)S(1)}, f32[2048]{0:T(1024)}, u32[]{:S(2)}) copy-start(f32[2048]{0:T(1024)} %param.26) | copy-start | bytes 24580
  0.6 3.8 %copy-start.16 = (f32[16,16,1,1]{1,0,3,2:T(8,128)S(1)}, f32[16,16,1,1]{1,0,3,2:T(8,128)}, u32[]{:S(2)}) copy-start(f32[16,16,1,1]{1,0,3,2:T(8,128)} %constant.237) | copy-start | bytes 3076
  2.2 3.2 %copy-start.18 = (f32[8,16,1,1]{1,0,3,2:T(8,128)S(1)}, f32[8,16,1,1]{1,0,3,2:T(8,128)}, u32[]{:S(2)}) copy-start(f32[8,16,1,1]{1,0,3,2:T(8,128)} %constant.239) | copy-start | bytes 1540
  4.5 1.5 copy-start.12
  4.5 8.6 %copy-start.5 = (s32[2048]{0:T(1024)S(1)}, s32[2048]{0:T(1024)}, u32[]{:S(2)}) copy-start(s32[2048]{0:T(1024)} %param.31) | copy-start | bytes 24580
  4.5 9.4 %copy-start.4 = (s32[2048]{0:T(1024)S(1)}, s32[2048]{0:T(1024)}, u32[]{:S(2)}) copy-start(s32[2048]{0:T(1024)} %param.30) | copy-start | bytes 24580
  6.0 52.6 %collective-permute-start = (f32[769,128]{1,0:T(8,128)S(1)}, f32[769,128]{1,0:T(8,128)S(1)}, u32[]{:S(2)}, u32[]{:S(2)}) collective-permute-start(f32[769,128]{1,0:T(8,128)S(1)} %pad_maximum_fusion.3), channel_id=1, source_target_pairs={{0,2},{2,4},{4,6},{6,8},{8,10},{10,12},{12,14},{14,16},{16,18},{18... | collective-permute-start | bytes 1181192 | tf_op jit(solution)/shard_map/ppermute | solution.py:24
  9.0 49.5 %collective-permute-start.1 = (f32[769,128]{1,0:T(8,128)S(1)}, f32[769,128]{1,0:T(8,128)S(1)}, u32[]{:S(2)}, u32[]{:S(2)}) collective-permute-start(f32[769,128]{1,0:T(8,128)S(1)} %pad_maximum_fusion.3), channel_id=1, source_target_pairs={{2,0},{4,2},{6,4},{8,6},{10,8},{12,10},{14,12},{16,14},{18,16},{20... | collective-permute-start | bytes 1181192 | tf_op jit(solution)/shard_map/ppermute | solution.py:26
  13.9 8.9 %copy-start.8 = (s32[2048]{0:T(1024)}, s32[2048]{0:T(1024)S(1)}, u32[]{:S(2)}) copy-start(s32[2048]{0:T(1024)S(1)} %get-tuple-element.97) | copy-start | bytes 24580
  14.8 39.3 %copy-start.6 = (s32[2048]{0:T(1024)}, s32[2048]{0:T(1024)S(1)}, u32[]{:S(2)}) copy-start(s32[2048]{0:T(1024)S(1)} %get-tuple-element.93) | copy-start | bytes 24580
  30.9 27.2 %copy-start.14 = (s32[4,128]{1,0:T(4,128)S(1)}, s32[4,128]{1,0:T(4,128)}, u32[]{:S(2)}) copy-start(s32[4,128]{1,0:T(4,128)} %param.24) | copy-start | bytes 6148
  31.0 27.2 %copy-start.20 = (s32[4,128]{1,0:T(4,128)S(1)}, s32[4,128]{1,0:T(4,128)}, u32[]{:S(2)}) copy-start(s32[4,128]{1,0:T(4,128)} %param.25) | copy-start | bytes 6148
  31.0 27.2 %copy-start.19 = (s32[2]{0:T(128)S(1)}, s32[2]{0:T(128)}, u32[]{:S(2)}) copy-start(s32[2]{0:T(128)} %constant.236.clone) | copy-start | bytes 28
  54.6 31.8 %all-to-all-start = ((f32[1,16,256]{2,0,1:T(1,128)}), f32[1,16,256]{2,0,1:T(1,128)S(1)}, u32[]{:S(2)}, u32[]{:S(2)}) async-start(f32[1,16,256]{2,0,1:T(1,128)} %bitcast.24), calls=%async_computation | async-start | bytes 32768 | tf_op jit(solution)/shard_map/all_to_all | solution.py:192
  58.5 3.6 %copy-start.3 = (f32[769,128]{1,0:T(8,128)}, f32[769,128]{1,0:T(8,128)S(1)}, u32[]{:S(2)}) copy-start(f32[769,128]{1,0:T(8,128)S(1)} %collective-permute-done.1) | copy-start | bytes 1181188
  66.2 3.1 %copy-start.17 = (f32[16,8,1,1]{0,1,3,2:T(8,128)S(1)}, f32[16,8,1,1]{0,1,3,2:T(8,128)}, u32[]{:S(2)}) copy-start(f32[16,8,1,1]{0,1,3,2:T(8,128)} %constant.240) | copy-start | bytes 1540
  66.2 3.1 %copy-start.23 = (f32[16]{0:T(128)S(1)}, f32[16]{0:T(128)}, u32[]{:S(2)}) copy-start(f32[16]{0:T(128)} %constant.235.clone) | copy-start | bytes 196
  70.2 0.9 copy-start.1
  83.9 9.5 %copy-start.13 = (f32[112,20]{0,1:T(8,128)S(1)}, f32[112,20]{0,1:T(8,128)}, u32[]{:S(2)}) copy-start(f32[112,20]{0,1:T(8,128)} %param.28) | copy-start | bytes 26884
  83.9 9.6 %copy-start.21 = (f32[112]{0:T(128)S(1)}, f32[112]{0:T(128)}, u32[]{:S(2)}) copy-start(f32[112]{0:T(128)} %param.29) | copy-start | bytes 1348
  83.9 9.7 %copy-start.22 = (f32[112]{0:T(128)S(1)}, f32[112]{0:T(128)}, u32[]{:S(2)}) copy-start(f32[112]{0:T(128)} %param.27) | copy-start | bytes 1348
  83.9 10.4 %copy-start.9 = (s32[2048]{0:T(1024)S(1)}, s32[2048]{0:T(1024)}, u32[]{:S(2)}) copy-start(s32[2048]{0:T(1024)} %copy-done.8) | copy-start | bytes 24580
  86.5 35.8 %all-to-all-start.1 = ((f32[80,16,256]{2,0,1:T(8,128)}), f32[80,16,256]{2,0,1:T(8,128)S(1)}, u32[]{:S(2)}, u32[]{:S(2)}) async-start(f32[80,16,256]{2,0,1:T(8,128)} %broadcast_select_fusion), calls=%async_computation.1 | async-start | bytes 2621440 | tf_op jit(solution)/shard_map/all_to_all | solution.py:191
  128.6 0.7 copy-start.11
  162.8 44.6 %copy-start.10 = (pred[4096]{0:T(1024)(128)(4,1)S(1)}, pred[4096]{0:T(1024)(128)(4,1)}, u32[]{:S(2)}) copy-start(pred[4096]{0:T(1024)(128)(4,1)} %compare_and_fusion.1) | copy-start | bytes 12292
  209.8 7.8 %copy-start.7 = (s32[2048]{0:T(1024)S(1)}, s32[2048]{0:T(1024)}, u32[]{:S(2)}) copy-start(s32[2048]{0:T(1024)} %copy-done.6) | copy-start | bytes 24580
  209.8 7.8 %copy-start.2 = (f32[24,4,16,128]{3,2,1,0:T(8,128)S(1)}, f32[24,4,16,128]{3,2,1,0:T(8,128)}, u32[]{:S(2)}) copy-start(f32[24,4,16,128]{3,2,1,0:T(8,128)} %copy-done.1) | copy-start | bytes 2359300
  209.9 8.8 %slice-start = ((f32[24,4,16,128]{3,2,1,0:T(8,128)}), f32[1,4,16,128]{3,2,1,0:T(8,128)S(1)}, s32[]{:S(2)}) async-start(f32[24,4,16,128]{3,2,1,0:T(8,128)} %copy-done.1), calls=%async_computation.5 | async-start | bytes 65536 | tf_op jit(solution)/shard_map/slice.28
  211.2 13.9 %all-to-all-start.4 = ((f32[16,4,256]{2,1,0:T(4,128)}), f32[16,4,256]{2,1,0:T(4,128)S(1)}, u32[]{:S(2)}, u32[]{:S(2)}) async-start(f32[16,4,256]{2,1,0:T(4,128)} %copy.119), calls=%async_computation.4 | async-start | bytes 131072 | tf_op jit(solution)/shard_map/all_to_all | solution.py:205
  218.8 12.8 %copy-start.15 = (pred[2048]{0:T(1024)(128)(4,1)S(1)}, pred[2048]{0:T(1024)(128)(4,1)}, u32[]{:S(2)}) copy-start(pred[2048]{0:T(1024)(128)(4,1)} %get-tuple-element.92) | copy-start | bytes 6148
